TPU v7x, 32 devices: a whole 2x2x4 slice. The times are simulated.
32 devices in a mesh: row: 2 (over y), col: 16 (over z, x, core).
Axes of the slice: x: 2, y: 2, z: 4, core: 2. Of those that a mesh axis runs over, the one named last changes fastest.
Arguments:
- blocks: bfloat16 [128, 2048, 128], P('row', 'col'), may hold values from -0.1875 to 0.1875
- block_rows: int32 [2, 1024], P('row', 'col'), may hold values from 0 to 2047, as said below
- block_cols: int32 [2, 1024], P('row', 'col'), may hold values from 0 to 255
- counts: int32 [2, 16], P('row', 'col'), may hold values from 1 to 64, as said below
- start_vectors: float32 [32, 524288], P(None, ('row', 'col')), may hold values from -6 to 6
Outputs:
- vectors: float32 [32, 524288], P(None, ('row', 'col'))
Inputs may be any that keep to these rules, and one draw needn't show every extreme that they name: counts[r, c] is the number of live slots of grid position (r, c); in every draw some position has all 64 slots live. For every grid position (r, c) and every o < 16, exactly 4 of its 64 slots have block_rows[r, c * 64 + s] // 128 == o.
All inputs are finite; a program needn't handle non-finite values.
Results may differ from a plain program's by a relative error of at most 0.0036.
Values may be sent and summed in bfloat16 or wider, within the bound.
A program may use at most 256 MiB of HBM per device.

v0:
```python
import math
import jax
import jax.numpy as jnp
from jax import lax
from jax.sharding import PartitionSpec as P

N = 524288
ITERS = 2


def cholesky_lower(gram_matrix):
    matrix_order = gram_matrix.shape[0]
    positions = jnp.arange(matrix_order)

    def column_step(position, factor):
        before = (positions < position).astype(gram_matrix.dtype)
        target_row = lax.dynamic_index_in_dim(factor, position, 0, keepdims=False) * before
        column = lax.dynamic_index_in_dim(gram_matrix, position, 1, keepdims=False)
        residue = column - jnp.sum(factor * target_row[None, :], axis=1)
        on_diagonal = positions == position
        pivot_value = jnp.sqrt(jnp.sum(jnp.where(on_diagonal, residue, 0.0)))
        values = jnp.where(on_diagonal, pivot_value, residue / pivot_value)
        values = jnp.where(positions >= position, values, 0.0)
        return lax.dynamic_update_index_in_dim(factor, values, position, 1)

    return lax.fori_loop(0, matrix_order, column_step, jnp.zeros_like(gram_matrix))


def lower_inverse(lower_factor):
    matrix_order = lower_factor.shape[0]
    positions = jnp.arange(matrix_order)

    def row_step(position, inverse):
        lower_row = lax.dynamic_index_in_dim(lower_factor, position, 0, keepdims=False)
        before = (positions < position).astype(lower_factor.dtype)
        inner_sum = jnp.sum((lower_row * before)[:, None] * inverse, axis=0)
        unit_row = (positions == position).astype(lower_factor.dtype)
        pivot_value = jnp.sum(lower_row * unit_row)
        return lax.dynamic_update_index_in_dim(
            inverse, (unit_row - inner_sum) / pivot_value, position, 0
        )

    return lax.fori_loop(0, matrix_order, row_step, jnp.zeros_like(lower_factor))


def accumulate(blocks, rows_index, cols_index, live_count, row_panel, col_panel):
    slot_count, block_size = (blocks.shape[0], blocks.shape[1])
    vector_count = row_panel.shape[0]
    row_blocks = row_panel.reshape(vector_count, -1, block_size)
    col_blocks = col_panel.reshape(vector_count, -1, block_size)
    group_size = math.gcd(slot_count, 64)
    turn_count = (live_count + group_size - 1) // group_size
    slot_offsets = jnp.arange(group_size, dtype=jnp.int32)

    def one_group(turn_index, partial_sums):
        row_sums, col_sums = partial_sums
        first_slot = turn_index * group_size
        live_mask = (first_slot + slot_offsets < live_count).astype(jnp.float32)
        from_cols = jnp.take(col_blocks, cols_index, axis=1)
        from_rows = jnp.take(row_blocks, rows_index, axis=1)
        to_cols = jnp.einsum("kgi,gij->kgj", from_rows, blocks, preferred_element_type=jnp.float32)
        col_sums = col_sums.at[:, cols_index].add(to_cols * live_mask[None, :, None])
        to_rows = jnp.einsum("kgj,gij->kgi", from_cols, blocks, preferred_element_type=jnp.float32)
        row_sums = row_sums.at[:, rows_index].add(to_rows * live_mask[None, :, None])
        return (row_sums, col_sums)

    row_start = jnp.zeros(row_blocks.shape, jnp.float32)
    initial = (row_start, jnp.zeros(col_blocks.shape, jnp.float32))
    return lax.fori_loop(0, turn_count, one_group, initial)


def per_device(blocks, block_rows, block_cols, counts, start_vectors):
    live_count = counts[0, 0]
    rows_index = block_rows[0]
    cols_index = block_cols[0]
    vectors = start_vectors
    for iteration in range(ITERS):
        rounded = vectors.astype(jnp.bfloat16)
        vector_count = rounded.shape[0]
        col_panel = lax.all_gather(rounded, "row", axis=1, tiled=True)
        row_panel = lax.all_gather(rounded, "col", axis=1, tiled=True)
        row_sums, col_sums = accumulate(
            blocks, rows_index, cols_index, live_count, row_panel, col_panel
        )
        from_row_group = lax.psum_scatter(
            row_sums.reshape(vector_count, -1), "col", scatter_dimension=1, tiled=True
        )
        from_col_group = lax.psum_scatter(
            col_sums.reshape(vector_count, -1), "row", scatter_dimension=1, tiled=True
        )
        product = from_row_group + from_col_group
        local_gram = jnp.dot(
            product, product.T, precision=lax.Precision.HIGHEST, preferred_element_type=jnp.float32
        )
        gram_matrix = lax.psum(local_gram, ("row", "col")) / N
        inverse = lower_inverse(cholesky_lower(gram_matrix))
        vectors = jnp.dot(
            inverse, product, precision=lax.Precision.HIGHEST, preferred_element_type=jnp.float32
        )
    return vectors


def solution(mesh):
    placed = (
        P("row", "col", None),
        P("row", "col"),
        P("row", "col"),
        P("row", "col"),
        P(None, ("row", "col")),
    )
    return jax.shard_map(
        per_device, mesh=mesh, in_specs=placed, out_specs=P(None, ("row", "col")), check_vma=False
    )
```

profile of v0, /device:TPU:0, one launch (start us, length us, event | category | flops | bytes accessed | tf_op | source)
XLA Modules:
  0.0 1549.7 jit_solution(5209276909103308987)
XLA Ops:
  6.5 2.8 convert_element_type.66
  11.0 34.4 %all-gather.5.cloned.1.call-done = bf16[32,32768]{1,0:T(8,128)(2,1)} async-done(((bf16[32,16384]{1,0:T(8,128)(2,1)}), bf16[32,32768]{1,0:T(8,128)(2,1)}) %all-gather.5.cloned.1.call-update) | async-done | bytes 2097168 | tf_op jit(solution)/shard_map/all_gather | solution.py:80
  45.4 3.3 copy_bitcast_fusion.7
  48.6 2.2 gather_fusion
  50.9 2.2 fusion.34
  53.1 121.4 %all-gather.7.cloned.1.call-done = bf16[32,262144]{1,0:T(8,128)(2,1)} async-done(((bf16[32,16384]{1,0:T(8,128)(2,1)}), bf16[32,262144]{1,0:T(8,128)(2,1)}) %all-gather.7.cloned.1.call-update) | async-done | bytes 16777232 | tf_op jit(solution)/shard_map/all_gather | solution.py:81
  174.5 14.5 copy_bitcast_fusion.3
  189.0 6.4 gather_fusion.1
  195.4 1.7 fusion.32
  197.1 11.3 broadcast.314.clone
  208.4 2.6 broadcast.315.clone
  210.9 20.4 %while.90 = (s32[]{:T(128)}, f32[32,2048,128]{2,0,1:T(8,128)}, f32[32,256,128]{2,0,1:T(8,128)}, s32[]{:T(128)}, s32[64]{0:T(128)S(1)}, /*index=5*/s32[]{:T(128)}...) while((s32[]{:T(128)}, f32[32,2048,128]{2,0,1:T(8,128)}, ...), condition=%wide.region_3.6_spmd.clone, body=%wide.region_0.5_spmd.clone.sunk | while | flops 1049155 | bytes 10487937 | solution.py:69
  211.6 2.7 broadcast_multiply_fusion.8
  214.3 9.0 scatter_fusion
  223.3 8.0 scatter_fusion.1
  231.3 4.4 copy_bitcast_fusion.5
  235.8 22.6 %copy_bitcast_fusion.1 = f32[32,262144]{1,0:T(8,128)} fusion(f32[32,2048,128]{2,0,1:T(8,128)} %get-tuple-element.609), kind=kLoop, calls=%fused_computation.69 | loop fusion | bytes 67108864 | tf_op jit(solution)/shard_map/reshape | solution.py:86
  258.5 30.0 %reduce-scatter.7.cloned.1.call-done = f32[32,16384]{1,0:T(8,128)} async-done(((f32[32,32768]{1,0:T(8,128)}), f32[32,16384]{1,0:T(8,128)}) %reduce-scatter.7.cloned.1.call-update) | async-done | bytes 2097168 | tf_op jit(solution)/shard_map/reduce_scatter | solution.py:88
  288.4 337.4 %reduce-scatter.5.cloned.1.call-done = f32[32,16384]{1,0:T(8,128)} async-done(((f32[32,262144]{1,0:T(8,128)}), f32[32,16384]{1,0:T(8,128)}) %reduce-scatter.5.cloned.1.call-update) | async-done | bytes 2097168 | tf_op jit(solution)/shard_map/reduce_scatter | solution.py:85
  625.8 2.4 add.220
  629.5 1.8 fusion.52
  631.3 39.1 %psum.14 = f32[32,32]{1,0:T(8,128)S(1)} all-reduce(f32[32,32]{1,0:T(8,128)S(1)} %fusion.52), channel_id=1, replica_groups=mesh['row'=2,'col'=16] {'row','col'}, use_global_device_ids=true, to_apply=%region_6.9 | all-reduce | flops 1024 | bytes 8192 | tf_op jit(solution)/shard_map/psum | solution.py:95
  670.4 58.1 %while.92 = (s32[]{:T(128)}, f32[32,32]{1,0:T(8,128)S(1)}, f32[32,32]{0,1:T(8,128)S(1)}, s32[]{:T(128)}, s32[]{:T(128)}) while((s32[]{:T(128)}, f32[32,32]{1,0:T(8,128)S(1)}, f32[32,32]{0,1:T(8,128)S(1)}, s32[]{:T(128)}, s32[]{:T(128)}) %tuple.192), condition=%wide.region_10.13_spmd.clone.clone, body=%wide.region_7.12_spmd.clone.clone.sunk | while | flops 2401 | bytes 8913 | solution.py:26
  728.6 49.0 %while.93 = (s32[]{:T(128)}, f32[32,32]{1,0:T(8,128)S(1)}, f32[32,32]{1,0:T(8,128)S(1)}, s32[]{:T(128)}, s32[]{:T(128)}) while((s32[]{:T(128)}, f32[32,32]{1,0:T(8,128)S(1)}, f32[32,32]{1,0:T(8,128)S(1)}, s32[]{:T(128)}, s32[]{:T(128)}) %tuple.195), condition=%wide.region_14.17_spmd.clone.clone, body=%wide.region_11.16_spmd.clone.clone.sunk | while | flops 2305 | bytes 6221 | solution.py:43
  777.6 4.4 convolution_convert_fusion
  782.8 32.2 %all-gather.9.cloned.1.call-done = bf16[32,32768]{1,0:T(8,128)(2,1)} async-done(((bf16[32,16384]{1,0:T(8,128)(2,1)}), bf16[32,32768]{1,0:T(8,128)(2,1)}) %all-gather.9.cloned.1.call-update) | async-done | bytes 2097168 | tf_op jit(solution)/shard_map/all_gather | solution.py:80
  815.1 3.3 copy_bitcast_fusion.6
  818.3 2.2 gather_fusion.2
  820.6 2.2 fusion.30
  822.8 121.5 %all-gather.11.cloned.1.call-done = bf16[32,262144]{1,0:T(8,128)(2,1)} async-done(((bf16[32,16384]{1,0:T(8,128)(2,1)}), bf16[32,262144]{1,0:T(8,128)(2,1)}) %all-gather.11.cloned.1.call-update) | async-done | bytes 16777232 | tf_op jit(solution)/shard_map/all_gather | solution.py:81
  944.3 14.5 copy_bitcast_fusion.2
  958.8 6.4 gather_fusion.3
  966.9 11.3 broadcast.314
  978.2 2.6 broadcast.315
  980.7 20.4 %while.91 = (s32[]{:T(128)}, f32[32,2048,128]{2,0,1:T(8,128)}, f32[32,256,128]{2,0,1:T(8,128)}, s32[]{:T(128)}, s32[64]{0:T(128)S(1)}, /*index=5*/s32[]{:T(128)}...) while((s32[]{:T(128)}, f32[32,2048,128]{2,0,1:T(8,128)}, ...), condition=%wide.region_18.21_spmd.clone, body=%wide.region_15.20_spmd.clone.sunk | while | flops 1049155 | bytes 10487937 | solution.py:69
  981.4 2.7 broadcast_multiply_fusion.9
  984.1 9.0 scatter_fusion.2
  993.1 8.0 scatter_fusion.3
  1001.1 4.4 copy_bitcast_fusion.4
  1005.6 22.6 %copy_bitcast_fusion = f32[32,262144]{1,0:T(8,128)} fusion(f32[32,2048,128]{2,0,1:T(8,128)} %get-tuple-element.613), kind=kLoop, calls=%fused_computation.68 | loop fusion | bytes 67108864 | tf_op jit(solution)/shard_map/reshape | solution.py:86
  1028.2 30.0 %reduce-scatter.11.cloned.1.call-done = f32[32,16384]{1,0:T(8,128)} async-done(((f32[32,32768]{1,0:T(8,128)}), f32[32,16384]{1,0:T(8,128)}) %reduce-scatter.11.cloned.1.call-update) | async-done | bytes 2097168 | tf_op jit(solution)/shard_map/reduce_scatter | solution.py:88
  1058.2 336.9 %reduce-scatter.9.cloned.1.call-done = f32[32,16384]{1,0:T(8,128)} async-done(((f32[32,262144]{1,0:T(8,128)}), f32[32,16384]{1,0:T(8,128)}) %reduce-scatter.9.cloned.1.call-update) | async-done | bytes 2097168 | tf_op jit(solution)/shard_map/reduce_scatter | solution.py:85
  1395.2 2.4 add.221
  1398.9 1.8 fusion.53
  1400.7 39.0 %psum.15 = f32[32,32]{1,0:T(8,128)S(1)} all-reduce(f32[32,32]{1,0:T(8,128)S(1)} %fusion.53), channel_id=1, replica_groups=mesh['row'=2,'col'=16] {'row','col'}, use_global_device_ids=true, to_apply=%region_21.24 | all-reduce | flops 1024 | bytes 8192 | tf_op jit(solution)/shard_map/psum | solution.py:95
  1439.8 53.9 %while.94 = (s32[]{:T(128)}, f32[32,32]{1,0:T(8,128)S(1)}, f32[32,32]{0,1:T(8,128)S(1)}, s32[]{:T(128)}, s32[]{:T(128)}) while((s32[]{:T(128)}, f32[32,32]{1,0:T(8,128)S(1)}, f32[32,32]{0,1:T(8,128)S(1)}, s32[]{:T(128)}, s32[]{:T(128)}) %tuple.201), condition=%wide.region_25.28_spmd.clone.clone, body=%wide.region_22.27_spmd.clone.clone.sunk | while | flops 2401 | bytes 8913 | solution.py:26
  1493.7 44.3 %while.95 = (s32[]{:T(128)}, f32[32,32]{1,0:T(8,128)S(1)}, f32[32,32]{1,0:T(8,128)S(1)}, s32[]{:T(128)}, s32[]{:T(128)}) while((s32[]{:T(128)}, f32[32,32]{1,0:T(8,128)S(1)}, f32[32,32]{1,0:T(8,128)S(1)}, s32[]{:T(128)}, s32[]{:T(128)}) %tuple.204), condition=%wide.region_29.32_spmd.clone.clone, body=%wide.region_26.31_spmd.clone.clone.sunk | while | flops 2305 | bytes 6221 | solution.py:43
  1538.1 4.8 fusion.54
  (685 shorter events, 164.6 us)
Async XLA Ops:
  6.5 44.4 %copy-start = (bf16[64,128,128]{2,1,0:T(8,128)(2,1)S(1)}, bf16[64,128,128]{2,1,0:T(8,128)(2,1)}, u32[]{:S(2)}) copy-start(bf16[64,128,128]{2,1,0:T(8,128)(2,1)} %param.21) | copy-start | bytes 6291460
  6.5 4.3 copy-start.3
  6.5 4.4 copy-start.4
  6.5 38.8 %all-gather.5.cloned.1.call-start = ((), (), s32[]{:S(2)}) async-start(), calls=%async_computation.4 | async-start | bytes 3145728 | tf_op jit(solution)/shard_map/all_gather | solution.py:80
  9.4 165.1 %all-gather.7.cloned.1.call-start = ((), (), s32[]{:S(2)}) async-start(), calls=%async_computation.5 | async-start | bytes 17825792 | tf_op jit(solution)/shard_map/all_gather | solution.py:81
  10.2 278.3 %reduce-scatter.7.cloned.1.call-start = ((), (), s32[]{:S(2)}) async-start(), calls=%async_computation.7 | async-start | bytes 6291456 | tf_op jit(solution)/shard_map/reduce_scatter | solution.py:88
  235.8 390.0 %reduce-scatter.5.cloned.1.call-start = ((), (), s32[]{:S(2)}) async-start(), calls=%async_computation.6 | async-start | bytes 35651584 | tf_op jit(solution)/shard_map/reduce_scatter | solution.py:85
  258.4 556.7 %all-gather.9.cloned.1.call-start = ((), (), s32[]{:S(2)}) async-start(), calls=%async_computation.8 | async-start | bytes 3145728 | tf_op jit(solution)/shard_map/all_gather | solution.py:80
  628.2 1.3 copy-start.2
  782.0 162.3 %all-gather.11.cloned.1.call-start = ((), (), s32[]{:S(2)}) async-start(), calls=%async_computation.9 | async-start | bytes 17825792 | tf_op jit(solution)/shard_map/all_gather | solution.py:81
  782.6 275.6 %reduce-scatter.11.cloned.1.call-start = ((), (), s32[]{:S(2)}) async-start(), calls=%async_computation.11 | async-start | bytes 6291456 | tf_op jit(solution)/shard_map/reduce_scatter | solution.py:88
  1005.6 389.6 %reduce-scatter.9.cloned.1.call-start = ((), (), s32[]{:S(2)}) async-start(), calls=%async_computation.10 | async-start | bytes 35651584 | tf_op jit(solution)/shard_map/reduce_scatter | solution.py:85
  1397.6 1.4 copy-start.1
Sparse Core Ops, SparseCore 0:
  9.5 35.8 all-gather.4
  47.6 126.9 all-gather.6
  235.9 52.4 reduce-scatter.6
  293.1 332.6 reduce-scatter.4
  782.1 32.8 all-gather.8
  817.4 126.9 all-gather.10
  1005.7 52.4 reduce-scatter.10
  1062.5 332.6 reduce-scatter.8
where the time goes:
time: 1550 us
  waiting for transfers between devices  1050 us (68%)
  other arithmetic  189 us (12%)
  local copies, waits for them, and re-layouts  153 us (10%)
  blocking collectives  78.1 us (5%)
  loops' own time  48.3 us (3%)
  matrix products  20.5 us (1%)
    reduce_scatter x2, waiting for transfers between devices, per_device(): lax.psum_scatter(row_sums.reshape(vector_count, -1), 'col', scatter_dimen...  674 us
    all_gather x2, waiting for transfers between devices, per_device(): row_panel = lax.all_gather(rounded, 'col', axis=1, tiled=True)  243 us
    psum x2, blocking collectives, per_device(): gram_matrix = lax.psum(local_gram, ('row', 'col')) / N  78.1 us
    all_gather x2, waiting for transfers between devices, per_device(): col_panel = lax.all_gather(rounded, 'row', axis=1, tiled=True)  66.7 us
    reduce_scatter x2, waiting for transfers between devices, per_device(): lax.psum_scatter(col_sums.reshape(vector_count, -1), 'row', scatter_dimen...  60 us
    another operation x2, loops' own time, cholesky_lower(): lax.fori_loop(0, matrix_order, column_step, jnp.zeros_like(gram_matrix))  46.9 us
    reshape x2, local copies, waits for them, and re-layouts, per_device(): row_sums.reshape(vector_count, -1)  45.2 us
    reduce_sum x64, other arithmetic, column_step(): pivot_value = jnp.sqrt(jnp.sum(jnp.where(on_diagonal, residue, 0.0)))  42.8 us
  transfers between devices with their start and end apart: 8, of which 8 were waited for; matrix products, arithmetic and copies ran while one was open for 4% of the time, Pallas kernels for 0%

commit v1 on v0

--- a/solution.py
+++ b/solution.py
@@ -1,3 +1,4 @@
+import functools
 import math
 import jax
 import jax.numpy as jnp
@@ -6,6 +7,14 @@
 
 N = 524288
 ITERS = 2
+
+
+def _guide_units(local_values, group_axis, ax_name):
+    f_next = lax.psum(lax.psum(local_values, group_axis), ax_name)
+    return f_next
+
+
+pass_samples_all_by_axis = functools.partial(_guide_units, group_axis="col", ax_name="row")
 
 
 def cholesky_lower(gram_matrix):
@@ -92,7 +101,7 @@
         local_gram = jnp.dot(
             product, product.T, precision=lax.Precision.HIGHEST, preferred_element_type=jnp.float32
         )
-        gram_matrix = lax.psum(local_gram, ("row", "col")) / N
+        gram_matrix = pass_samples_all_by_axis(local_gram) / N
         inverse = lower_inverse(cholesky_lower(gram_matrix))
         vectors = jnp.dot(
             inverse, product, precision=lax.Precision.HIGHEST, preferred_element_type=jnp.float32

time: 1550 us -> 1610 us (1.039)
  blocking collectives: 78.1 us -> 135 us
    psum x2 -> x4, blocking collectives: 78.1 us -> 135 us  [_guide_units(): f_next = lax.psum(lax.psum(local_values, group_axis), ax_name)]
where the time goes in v1:
time: 1610 us; the launch traced here: 1600 us
  waiting for transfers between devices  1040 us (65%)
  other arithmetic  189 us (12%)
  local copies, waits for them, and re-layouts  153 us (10%)
  blocking collectives  135 us (8%)
  loops' own time  48.3 us (3%)
  matrix products  20.5 us (1%)
    reduce_scatter x2, waiting for transfers between devices, per_device(): lax.psum_scatter(row_sums.reshape(vector_count, -1), 'col', scatter_dimen...  674 us
    all_gather x2, waiting for transfers between devices, per_device(): row_panel = lax.all_gather(rounded, 'col', axis=1, tiled=True)  243 us
    psum x4, blocking collectives, _guide_units(): f_next = lax.psum(lax.psum(local_values, group_axis), ax_name)  135 us
    all_gather x2, waiting for transfers between devices, per_device(): col_panel = lax.all_gather(rounded, 'row', axis=1, tiled=True)  63.2 us
    reduce_scatter x2, waiting for transfers between devices, per_device(): lax.psum_scatter(col_sums.reshape(vector_count, -1), 'row', scatter_dimen...  60 us
    another operation x2, loops' own time, cholesky_lower(): lax.fori_loop(0, matrix_order, column_step, jnp.zeros_like(gram_matrix))  46.9 us
    reshape x2, local copies, waits for them, and re-layouts, per_device(): row_sums.reshape(vector_count, -1)  45.2 us
    reduce_sum x64, other arithmetic, column_step(): pivot_value = jnp.sqrt(jnp.sum(jnp.where(on_diagonal, residue, 0.0)))  42.8 us
  transfers between devices with their start and end apart: 8, of which 8 were waited for; matrix products, arithmetic and copies ran while one was open for 4% of the time, Pallas kernels for 0%

profile of v1, /device:TPU:0, one launch (start us, length us, event | category | flops | bytes accessed | tf_op | source)
XLA Modules:
  0.0 1603.6 jit_solution(4482185751931948693)
XLA Ops:
  6.5 2.8 convert_element_type.66
  11.0 34.4 %all-gather.5.cloned.1.call-done = bf16[32,32768]{1,0:T(8,128)(2,1)} async-done(((bf16[32,16384]{1,0:T(8,128)(2,1)}), bf16[32,32768]{1,0:T(8,128)(2,1)}) %all-gather.5.cloned.1.call-update) | async-done | bytes 2097168 | tf_op jit(solution)/shard_map/all_gather | solution.py:89
  45.4 3.3 copy_bitcast_fusion.7
  48.6 2.2 gather_fusion
  50.9 2.2 fusion.34
  53.1 121.4 %all-gather.7.cloned.1.call-done = bf16[32,262144]{1,0:T(8,128)(2,1)} async-done(((bf16[32,16384]{1,0:T(8,128)(2,1)}), bf16[32,262144]{1,0:T(8,128)(2,1)}) %all-gather.7.cloned.1.call-update) | async-done | bytes 16777232 | tf_op jit(solution)/shard_map/all_gather | solution.py:90
  174.5 14.5 copy_bitcast_fusion.3
  189.0 6.4 gather_fusion.1
  197.1 11.3 broadcast.314.clone
  208.4 2.6 broadcast.315.clone
  210.9 20.4 %while.90 = (s32[]{:T(128)}, f32[32,2048,128]{2,0,1:T(8,128)}, f32[32,256,128]{2,0,1:T(8,128)}, s32[]{:T(128)}, s32[64]{0:T(128)S(1)}, /*index=5*/s32[]{:T(128)}...) while((s32[]{:T(128)}, f32[32,2048,128]{2,0,1:T(8,128)}, ...), condition=%wide.region_3.6_spmd.clone, body=%wide.region_0.5_spmd.clone.sunk | while | flops 1049155 | bytes 10487937 | solution.py:78
  211.6 2.7 broadcast_multiply_fusion.8
  214.3 9.0 scatter_fusion
  223.3 8.0 scatter_fusion.1
  231.3 4.4 copy_bitcast_fusion.5
  235.8 22.6 %copy_bitcast_fusion.1 = f32[32,262144]{1,0:T(8,128)} fusion(f32[32,2048,128]{2,0,1:T(8,128)} %get-tuple-element.609), kind=kLoop, calls=%fused_computation.69 | loop fusion | bytes 67108864 | tf_op jit(solution)/shard_map/reshape | solution.py:95
  258.5 30.0 %reduce-scatter.7.cloned.1.call-done = f32[32,16384]{1,0:T(8,128)} async-done(((f32[32,32768]{1,0:T(8,128)}), f32[32,16384]{1,0:T(8,128)}) %reduce-scatter.7.cloned.1.call-update) | async-done | bytes 2097168 | tf_op jit(solution)/shard_map/reduce_scatter | solution.py:97
  288.4 337.4 %reduce-scatter.5.cloned.1.call-done = f32[32,16384]{1,0:T(8,128)} async-done(((f32[32,262144]{1,0:T(8,128)}), f32[32,16384]{1,0:T(8,128)}) %reduce-scatter.5.cloned.1.call-update) | async-done | bytes 2097168 | tf_op jit(solution)/shard_map/reduce_scatter | solution.py:94
  625.8 2.4 add.224
  629.5 1.8 fusion.52
  631.3 59.6 %psum.28 = f32[32,32]{1,0:T(8,128)S(1)} all-reduce(f32[32,32]{1,0:T(8,128)S(1)} %fusion.52), channel_id=1, replica_groups=mesh['row'=2,'col'=16] {'col'}, use_global_device_ids=true, to_apply=%region_6.9 | all-reduce | flops 1024 | bytes 8192 | tf_op jit(solution)/shard_map/psum | solution.py:13
  690.9 8.1 psum.29
  699.1 58.1 %while.92 = (s32[]{:T(128)}, f32[32,32]{1,0:T(8,128)S(1)}, f32[32,32]{0,1:T(8,128)S(1)}, s32[]{:T(128)}, s32[]{:T(128)}) while((s32[]{:T(128)}, f32[32,32]{1,0:T(8,128)S(1)}, f32[32,32]{0,1:T(8,128)S(1)}, s32[]{:T(128)}, s32[]{:T(128)}) %tuple.192), condition=%wide.region_11.14_spmd.clone.clone, body=%wide.region_8.13_spmd.clone.clone.sunk | while | flops 2401 | bytes 8913 | solution.py:35
  757.3 49.0 %while.93 = (s32[]{:T(128)}, f32[32,32]{1,0:T(8,128)S(1)}, f32[32,32]{1,0:T(8,128)S(1)}, s32[]{:T(128)}, s32[]{:T(128)}) while((s32[]{:T(128)}, f32[32,32]{1,0:T(8,128)S(1)}, f32[32,32]{1,0:T(8,128)S(1)}, s32[]{:T(128)}, s32[]{:T(128)}) %tuple.195), condition=%wide.region_15.18_spmd.clone.clone, body=%wide.region_12.17_spmd.clone.clone.sunk | while | flops 2305 | bytes 6221 | solution.py:52
  806.2 4.4 convolution_convert_fusion
  811.5 28.8 %all-gather.9.cloned.1.call-done = bf16[32,32768]{1,0:T(8,128)(2,1)} async-done(((bf16[32,16384]{1,0:T(8,128)(2,1)}), bf16[32,32768]{1,0:T(8,128)(2,1)}) %all-gather.9.cloned.1.call-update) | async-done | bytes 2097168 | tf_op jit(solution)/shard_map/all_gather | solution.py:89
  840.3 3.3 copy_bitcast_fusion.6
  843.6 2.2 gather_fusion.2
  845.8 2.2 fusion.30
  848.0 121.5 %all-gather.11.cloned.1.call-done = bf16[32,262144]{1,0:T(8,128)(2,1)} async-done(((bf16[32,16384]{1,0:T(8,128)(2,1)}), bf16[32,262144]{1,0:T(8,128)(2,1)}) %all-gather.11.cloned.1.call-update) | async-done | bytes 16777232 | tf_op jit(solution)/shard_map/all_gather | solution.py:90
  969.5 14.5 copy_bitcast_fusion.2
  984.0 6.4 gather_fusion.3
  992.1 11.3 broadcast.314
  1003.4 2.6 broadcast.315
  1006.0 20.4 %while.91 = (s32[]{:T(128)}, f32[32,2048,128]{2,0,1:T(8,128)}, f32[32,256,128]{2,0,1:T(8,128)}, s32[]{:T(128)}, s32[64]{0:T(128)S(1)}, /*index=5*/s32[]{:T(128)}...) while((s32[]{:T(128)}, f32[32,2048,128]{2,0,1:T(8,128)}, ...), condition=%wide.region_19.22_spmd.clone, body=%wide.region_16.21_spmd.clone.sunk | while | flops 1049155 | bytes 10487937 | solution.py:78
  1006.6 2.7 broadcast_multiply_fusion.9
  1009.3 9.0 scatter_fusion.2
  1018.3 8.0 scatter_fusion.3
  1026.3 4.4 copy_bitcast_fusion.4
  1030.8 22.6 %copy_bitcast_fusion = f32[32,262144]{1,0:T(8,128)} fusion(f32[32,2048,128]{2,0,1:T(8,128)} %get-tuple-element.613), kind=kLoop, calls=%fused_computation.68 | loop fusion | bytes 67108864 | tf_op jit(solution)/shard_map/reshape | solution.py:95
  1053.4 30.0 %reduce-scatter.11.cloned.1.call-done = f32[32,16384]{1,0:T(8,128)} async-done(((f32[32,32768]{1,0:T(8,128)}), f32[32,16384]{1,0:T(8,128)}) %reduce-scatter.11.cloned.1.call-update) | async-done | bytes 2097168 | tf_op jit(solution)/shard_map/reduce_scatter | solution.py:97
  1083.4 336.9 %reduce-scatter.9.cloned.1.call-done = f32[32,16384]{1,0:T(8,128)} async-done(((f32[32,262144]{1,0:T(8,128)}), f32[32,16384]{1,0:T(8,128)}) %reduce-scatter.9.cloned.1.call-update) | async-done | bytes 2097168 | tf_op jit(solution)/shard_map/reduce_scatter | solution.py:94
  1420.4 2.4 add.225
  1425.9 59.6 %psum.30 = f32[32,32]{1,0:T(8,128)S(1)} all-reduce(f32[32,32]{1,0:T(8,128)S(1)} %fusion.53), channel_id=1, replica_groups=mesh['row'=2,'col'=16] {'col'}, use_global_device_ids=true, to_apply=%region_22.25 | all-reduce | flops 1024 | bytes 8192 | tf_op jit(solution)/shard_map/psum | solution.py:13
  1485.5 8.1 psum.31
  1493.7 53.9 %while.94 = (s32[]{:T(128)}, f32[32,32]{1,0:T(8,128)S(1)}, f32[32,32]{0,1:T(8,128)S(1)}, s32[]{:T(128)}, s32[]{:T(128)}) while((s32[]{:T(128)}, f32[32,32]{1,0:T(8,128)S(1)}, f32[32,32]{0,1:T(8,128)S(1)}, s32[]{:T(128)}, s32[]{:T(128)}) %tuple.201), condition=%wide.region_27.30_spmd.clone.clone, body=%wide.region_24.29_spmd.clone.clone.sunk | while | flops 2401 | bytes 8913 | solution.py:35
  1547.7 44.3 %while.95 = (s32[]{:T(128)}, f32[32,32]{1,0:T(8,128)S(1)}, f32[32,32]{1,0:T(8,128)S(1)}, s32[]{:T(128)}, s32[]{:T(128)}) while((s32[]{:T(128)}, f32[32,32]{1,0:T(8,128)S(1)}, f32[32,32]{1,0:T(8,128)S(1)}, s32[]{:T(128)}, s32[]{:T(128)}) %tuple.204), condition=%wide.region_31.34_spmd.clone.clone, body=%wide.region_28.33_spmd.clone.clone.sunk | while | flops 2305 | bytes 6221 | solution.py:52
  1592.0 4.8 fusion.54
  (687 shorter events, 168.1 us)
Async XLA Ops:
  6.5 44.4 %copy-start = (bf16[64,128,128]{2,1,0:T(8,128)(2,1)S(1)}, bf16[64,128,128]{2,1,0:T(8,128)(2,1)}, u32[]{:S(2)}) copy-start(bf16[64,128,128]{2,1,0:T(8,128)(2,1)} %param.21) | copy-start | bytes 6291460
  6.5 4.3 copy-start.3
  6.5 4.4 copy-start.4
  6.5 38.8 %all-gather.5.cloned.1.call-start = ((), (), s32[]{:S(2)}) async-start(), calls=%async_computation.4 | async-start | bytes 3145728 | tf_op jit(solution)/shard_map/all_gather | solution.py:89
  9.4 165.1 %all-gather.7.cloned.1.call-start = ((), (), s32[]{:S(2)}) async-start(), calls=%async_computation.5 | async-start | bytes 17825792 | tf_op jit(solution)/shard_map/all_gather | solution.py:90
  10.2 278.3 %reduce-scatter.7.cloned.1.call-start = ((), (), s32[]{:S(2)}) async-start(), calls=%async_computation.7 | async-start | bytes 6291456 | tf_op jit(solution)/shard_map/reduce_scatter | solution.py:97
  235.8 390.0 %reduce-scatter.5.cloned.1.call-start = ((), (), s32[]{:S(2)}) async-start(), calls=%async_computation.6 | async-start | bytes 35651584 | tf_op jit(solution)/shard_map/reduce_scatter | solution.py:94
  258.4 581.9 %all-gather.9.cloned.1.call-start = ((), (), s32[]{:S(2)}) async-start(), calls=%async_computation.8 | async-start | bytes 3145728 | tf_op jit(solution)/shard_map/all_gather | solution.py:89
  628.2 1.3 copy-start.2
  810.7 158.8 %all-gather.11.cloned.1.call-start = ((), (), s32[]{:S(2)}) async-start(), calls=%async_computation.9 | async-start | bytes 17825792 | tf_op jit(solution)/shard_map/all_gather | solution.py:90
  811.3 272.2 %reduce-scatter.11.cloned.1.call-start = ((), (), s32[]{:S(2)}) async-start(), calls=%async_computation.11 | async-start | bytes 6291456 | tf_op jit(solution)/shard_map/reduce_scatter | solution.py:97
  1030.8 389.6 %reduce-scatter.9.cloned.1.call-start = ((), (), s32[]{:S(2)}) async-start(), calls=%async_computation.10 | async-start | bytes 35651584 | tf_op jit(solution)/shard_map/reduce_scatter | solution.py:94
  1422.8 1.4 copy-start.1
Sparse Core Ops, SparseCore 0:
  9.5 35.8 all-gather.4
  47.6 126.9 all-gather.6
  235.9 52.4 reduce-scatter.6
  293.1 332.6 reduce-scatter.4
  810.8 29.4 all-gather.8
  842.6 126.9 all-gather.10
  1030.9 52.4 reduce-scatter.10
  1087.7 332.6 reduce-scatter.8
